TPU v7x, 256 devices: a whole 4x4x8 slice. The times are simulated.
256 devices in a mesh: ctx: 8 (over x, core), ch: 32 (over y, z).
Axes of the slice: x: 4, y: 4, z: 8, core: 2. Of those that a mesh axis runs over, the one named last changes fastest.
Arguments:
- out_grad: bfloat16 [2048, 8192], P('ctx', 'ch'), may hold values from -6 to 6
- out_weight: bfloat16 [8192, 8192], P(None, 'ch'), may hold values from -0.125 to 0.125
- query_in: bfloat16 [2048, 8192], P('ctx', 'ch'), may hold values from -6 to 6
- conv_out: bfloat16 [2048, 8192], P('ctx', 'ch'), may hold values from -6 to 6
- residues: float32 [8192, 16], P('ch'), may hold values from -0.3 to 0.3
- decay_rates: float32 [8192, 16], P('ch'), may hold values from 0.96 to 1, as said below
Outputs:
- grad_query: bfloat16 [2048, 8192], P('ctx', 'ch')
- grad_input: bfloat16 [2048, 8192], P('ctx', 'ch')
Inputs may be any that keep to these rules, and one draw needn't show every extreme that they name: `decay_rates`: each pole lies strictly below 1.
All inputs are finite; a program needn't handle non-finite values.
Results may differ from a plain program's by a relative error of at most 0.001.
Values may be sent and summed in bfloat16 or wider, within the bound.
A program may use at most 128 MiB of HBM per device.

v0:
```python
import math

import jax
import jax.numpy as jnp
from jax import lax
from jax.sharding import PartitionSpec as P


def from_behind(shard, axis, by):
    length = lax.axis_size(axis)
    pairs = [(i, i + by) for i in range(length) if 0 <= i + by < length]
    return lax.ppermute(shard, axis, pairs)


def local(out_grad, out_weight, query_in, conv_out, residues, decay_rates):
    tok_rows = out_grad.shape[0]
    width_local = query_in.shape[1]
    highest = lax.Precision.HIGHEST
    grad_mix = lax.psum_scatter(
        lax.dot_general(
            out_weight, out_grad, (((1,), (1,)), ((), ())), preferred_element_type=jnp.float32
        ),
        "ch",
        scatter_dimension=0,
        tiled=True,
    ).T
    grad_query = (grad_mix * conv_out.astype(jnp.float32)).astype(jnp.bfloat16)
    grad_conv = grad_mix * query_in.astype(jnp.float32)
    block_len = math.gcd(tok_rows, 128)
    block_count = tok_rows // block_len
    log_decay = jnp.log(decay_rates)
    offsets = jnp.arange(block_len, dtype=jnp.float32)
    powers = jnp.exp(offsets[:, None, None] * log_decay[None])
    filter_taps = jnp.sum(residues[None] * powers, axis=2)
    lagged = jnp.arange(block_len)[None, :] - jnp.arange(block_len)[:, None]
    toeplitz = jnp.where(
        (lagged >= 0)[:, :, None], jnp.take(filter_taps, jnp.maximum(lagged, 0), axis=0), 0.0
    )
    blocks = grad_conv.reshape(block_count, block_len, width_local)
    inner_part = jnp.einsum("stc,btc->bsc", toeplitz, blocks, precision=highest)
    block_sums = jnp.einsum("btc,tcn->bcn", blocks, powers, precision=highest)
    decay_block = jnp.exp(block_len * log_decay)

    def carry_back(late_state, block_sum):
        return (decay_block * late_state + block_sum, late_state)

    zero_state = jnp.zeros(decay_rates.shape, jnp.float32)
    first_state, ends_local = lax.scan(carry_back, zero_state, block_sums, reverse=True)
    decay_group = jnp.exp(tok_rows * log_decay)

    def hop_once(hop_index, received):
        return from_behind(decay_group * received + first_state, "ctx", -1)

    incoming = lax.fori_loop(0, lax.axis_size("ctx") - 1, hop_once, zero_state)
    remaining = jnp.exp(
        (block_count - 1 - jnp.arange(block_count, dtype=jnp.float32))[:, None, None]
        * block_len
        * log_decay[None]
    )
    block_ends = ends_local + remaining * incoming[None]
    tail_weights = jnp.exp((block_len - offsets)[:, None, None] * log_decay[None]) * residues[None]
    outer_part = jnp.einsum("scn,bcn->bsc", tail_weights, block_ends, precision=highest)
    grad_input = (inner_part + outer_part).reshape(tok_rows, width_local).astype(jnp.bfloat16)
    return (grad_query, grad_input)


def solution(mesh):
    placed = (
        P("ctx", "ch"),
        P(None, "ch"),
        P("ctx", "ch"),
        P("ctx", "ch"),
        P("ch", None),
        P("ch", None),
    )
    return jax.shard_map(
        local,
        mesh=mesh,
        in_specs=placed,
        out_specs=(P("ctx", "ch"), P("ctx", "ch")),
        check_vma=False,
    )
```

profile of v0, /device:TPU:1, one launch (start us, length us, event | category | flops | bytes accessed | tf_op | source)
XLA Modules:
  0.0 328.3 jit_solution(11594522040229895536)
XLA Ops:
  7.2 0.0 copy-start
  7.2 0.0 reduce-scatter.2.cloned.1.call-start
  7.2 0.8 copy-done
  8.1 6.7 %fusion.30 = f32[8192,256]{1,0:T(8,128)} fusion(bf16[8192,256]{1,0:T(8,128)(2,1)} %param.11, bf16[256,256]{1,0:T(8,128)(2,1)S(1)} %copy-done), kind=kOutput, calls=%fused_computation.40 | convolution fusion | flops 1073741824 | bytes 12713984 | tf_op jit(solution)/shard_map/dot_general | solution.py:20
  14.7 0.0 copy-start.1
  14.8 0.0 copy-start.2
  14.8 0.0 copy-start.4
  14.8 0.0 copy-start.3
  14.8 0.0 reduce-scatter.2.cloned.1.call-update
  14.8 0.9 copy-done.1
  15.7 0.1 copy.27
  15.8 0.0 copy-done.2
  15.8 0.1 copy.26
  15.9 0.0 copy-done.4
  15.9 0.1 copy.29
  16.0 0.0 copy-done.3
  16.0 0.1 copy.28
  16.1 1.7 multiply_reduce_fusion
  17.8 0.1 copy.30
  17.9 62.0 %gather_fusion = f32[16384,256]{1,0:T(8,128)} fusion(f32[128,256]{1,0:T(8,128)S(1)} %copy.30, s32[16384]{0:T(1024)S(1)} %bitcast_clamp_fusion), kind=kCustom, calls=%fused_computation | custom fusion | bytes 33619968 | tf_op jit(solution)/shard_map/jit(_take)/gather | solution.py:37
  80.0 18.1 %copy.31 = f32[128,128,256]{1,0,2:T(8,128)} copy(f32[128,128,256]{2,1,0:T(8,128)} %bitcast.28) | data formatting | bytes 33554432 | tf_op jit(solution)/shard_map/jit(_take)/gather | solution.py:37
  98.2 145.7 %reduce-scatter.2.cloned.1.call-done = f32[256,256]{1,0:T(8,128)} async-done(((f32[8192,256]{1,0:T(8,128)}), f32[256,256]{1,0:T(8,128)}) %reduce-scatter.2.cloned.1.call-update) | async-done | bytes 262160 | tf_op jit(solution)/shard_map/reduce_scatter | solution.py:19
  243.9 1.0 bitcast_multiply_fusion
  244.9 0.8 copy.34
  245.6 0.1 reshape.65
  245.8 3.5 %fusion.12 = f32[2,256,16]{2,0,1:T(2,128)S(1)} fusion(f32[2,128,256]{1,0,2:T(2,128)S(1)} %reshape.65, f32[256,16]{1,0:T(8,128)S(1)} %copy.29), kind=kOutput, calls=%fused_computation.18 | convolution fusion | flops 13107200 | bytes 311296 | tf_op jit(solution)/shard_map/btc,tcn->bcn/dot_general | solution.py:41
  249.3 0.1 copy.32
  249.4 0.1 while.28
  249.5 39.3 %while.27 = (s32[]{:T(128)}, f32[256,16]{0,1:T(8,128)S(1)}, f32[256,16]{0,1:T(8,128)S(1)}, f32[256,16]{0,1:T(8,128)S(1)}, s32[]{:T(128)}) while((s32[]{:T(128)}, f32[256,16]{0,1:T(8,128)S(1)}, f32[256,16]{0,1:T(8,128)S(1)}, f32[256,16]{0,1:T(8,128)S(1)}, s32[]{:T(128)}) %tuple.68), condition=%wide.region_5.6_spmd, body=%wide.region_4.5_spmd.sunk | while | flops 8194 | bytes 131173 | solution.py:54
  249.5 6.5 %collective-permute-start = (f32[256,16]{0,1:T(8,128)S(1)}, f32[256,16]{0,1:T(8,128)S(1)}, u32[]{:S(2)}, u32[]{:S(2)}) collective-permute-start(f32[256,16]{0,1:T(8,128)S(1)} %multiply_add_fusion.3), channel_id=1, source_target_pairs={{32,0},{64,32},{96,64},{128,96},{160,128},{192,160},{224,192},{33,... | collective-permute-start | bytes 49160 | tf_op jit(solution)/shard_map/while/body/eval_jaxpr/ppermute | solution.py:12
  256.0 2.5 collective-permute-done
  258.5 1.9 collective-permute-start
  260.4 3.1 collective-permute-done
  263.6 1.9 collective-permute-start
  265.5 3.1 collective-permute-done
  268.6 1.9 collective-permute-start
  270.5 3.1 collective-permute-done
  273.7 1.9 collective-permute-start
  275.6 3.1 collective-permute-done
  278.7 1.9 collective-permute-start
  280.7 3.1 collective-permute-done
  283.8 1.9 collective-permute-start
  285.7 3.1 collective-permute-done
  288.8 0.1 multiply_add_fusion.1
  288.9 0.1 copy.33
  289.1 28.7 %fusion = f32[256,2,128]{2,1,0:T(2,128)S(1)} fusion(f32[2,128,256]{1,0,2:T(2,128)S(1)} %reshape.65, f32[128,128,256]{1,0,2:T(8,128)} %copy.31, pred[128,128]{1,0:T(8,128)(4,1)S(1)} %get-tuple-element.193, pred[128,128]{1,0:T(8,128)(4,1)S(1)} %get-tuple-element.194), kind=kOutput, calls=%fused_computation.4 | convolution fusion | flops 109051904 | bytes 17334272 | tf_op jit(solution)/shard_map/stc,btc->bsc/dot_general | solution.py:40
  317.8 2.9 fusion.19
  320.6 0.8 copy.36
  (19 shorter events, 0.2 us)
Async XLA Ops:
  7.2 0.9 copy-start
  7.2 236.7 %reduce-scatter.2.cloned.1.call-start = ((), (), s32[]{:S(2)}) async-start(), calls=%async_computation.1 | async-start | bytes 8650752 | tf_op jit(solution)/shard_map/reduce_scatter | solution.py:19
  14.7 0.9 copy-start.1
  14.8 1.0 copy-start.2
  14.8 1.1 copy-start.4
  14.8 1.3 copy-start.3
  249.5 9.0 %collective-permute-start = (f32[256,16]{0,1:T(8,128)S(1)}, f32[256,16]{0,1:T(8,128)S(1)}, u32[]{:S(2)}, u32[]{:S(2)}) collective-permute-start(f32[256,16]{0,1:T(8,128)S(1)} %multiply_add_fusion.3), channel_id=1, source_target_pairs={{32,0},{64,32},{96,64},{128,96},{160,128},{192,160},{224,192},{33,... | collective-permute-start | bytes 49160 | tf_op jit(solution)/shard_map/while/body/eval_jaxpr/ppermute | solution.py:12
  258.5 5.0 %collective-permute-start = (f32[256,16]{0,1:T(8,128)S(1)}, f32[256,16]{0,1:T(8,128)S(1)}, u32[]{:S(2)}, u32[]{:S(2)}) collective-permute-start(f32[256,16]{0,1:T(8,128)S(1)} %multiply_add_fusion.3), channel_id=1, source_target_pairs={{32,0},{64,32},{96,64},{128,96},{160,128},{192,160},{224,192},{33,... | collective-permute-start | bytes 49160 | tf_op jit(solution)/shard_map/while/body/eval_jaxpr/ppermute | solution.py:12
  263.6 5.0 %collective-permute-start = (f32[256,16]{0,1:T(8,128)S(1)}, f32[256,16]{0,1:T(8,128)S(1)}, u32[]{:S(2)}, u32[]{:S(2)}) collective-permute-start(f32[256,16]{0,1:T(8,128)S(1)} %multiply_add_fusion.3), channel_id=1, source_target_pairs={{32,0},{64,32},{96,64},{128,96},{160,128},{192,160},{224,192},{33,... | collective-permute-start | bytes 49160 | tf_op jit(solution)/shard_map/while/body/eval_jaxpr/ppermute | solution.py:12
  268.6 5.0 %collective-permute-start = (f32[256,16]{0,1:T(8,128)S(1)}, f32[256,16]{0,1:T(8,128)S(1)}, u32[]{:S(2)}, u32[]{:S(2)}) collective-permute-start(f32[256,16]{0,1:T(8,128)S(1)} %multiply_add_fusion.3), channel_id=1, source_target_pairs={{32,0},{64,32},{96,64},{128,96},{160,128},{192,160},{224,192},{33,... | collective-permute-start | bytes 49160 | tf_op jit(solution)/shard_map/while/body/eval_jaxpr/ppermute | solution.py:12
  273.7 5.0 %collective-permute-start = (f32[256,16]{0,1:T(8,128)S(1)}, f32[256,16]{0,1:T(8,128)S(1)}, u32[]{:S(2)}, u32[]{:S(2)}) collective-permute-start(f32[256,16]{0,1:T(8,128)S(1)} %multiply_add_fusion.3), channel_id=1, source_target_pairs={{32,0},{64,32},{96,64},{128,96},{160,128},{192,160},{224,192},{33,... | collective-permute-start | bytes 49160 | tf_op jit(solution)/shard_map/while/body/eval_jaxpr/ppermute | solution.py:12
  278.7 5.0 %collective-permute-start = (f32[256,16]{0,1:T(8,128)S(1)}, f32[256,16]{0,1:T(8,128)S(1)}, u32[]{:S(2)}, u32[]{:S(2)}) collective-permute-start(f32[256,16]{0,1:T(8,128)S(1)} %multiply_add_fusion.3), channel_id=1, source_target_pairs={{32,0},{64,32},{96,64},{128,96},{160,128},{192,160},{224,192},{33,... | collective-permute-start | bytes 49160 | tf_op jit(solution)/shard_map/while/body/eval_jaxpr/ppermute | solution.py:12
  283.8 5.0 %collective-permute-start = (f32[256,16]{0,1:T(8,128)S(1)}, f32[256,16]{0,1:T(8,128)S(1)}, u32[]{:S(2)}, u32[]{:S(2)}) collective-permute-start(f32[256,16]{0,1:T(8,128)S(1)} %multiply_add_fusion.3), channel_id=1, source_target_pairs={{32,0},{64,32},{96,64},{128,96},{160,128},{192,160},{224,192},{33,... | collective-permute-start | bytes 49160 | tf_op jit(solution)/shard_map/while/body/eval_jaxpr/ppermute | solution.py:12
Sparse Core Ops, SparseCore 0:
  14.9 228.9 reduce-scatter.1
where the time goes:
time: 329 us; the launch traced here: 328 us
  waiting for transfers between devices  167 us (51%)
  local copies, waits for them, and re-layouts  84.3 us (26%)
  matrix products  41.8 us (13%)
  starting transfers between devices  18 us (5%)
  between operations  14.2 us (4%)
    reduce_scatter x1, waiting for transfers between devices, local(): lax.psum_scatter(lax.dot_general(out_weight, out_grad, (((1,), (1,)), (()...  146 us
    gather x2, local copies, waits for them, and re-layouts, local(): jnp.take(filter_taps, jnp.maximum(lagged, 0), axis=0)  80.2 us
    dot_general x1, matrix products, local(): inner_part = jnp.einsum('stc,btc->bsc', toeplitz, blocks, precision=highest)  28.7 us
    ppermute x7, waiting for transfers between devices, from_behind(): return lax.ppermute(shard, axis, pairs)  21.2 us
    ppermute x7, starting transfers between devices, from_behind(): return lax.ppermute(shard, axis, pairs)  17.9 us
    dot_general x1, matrix products, local(): lax.dot_general(out_weight, out_grad, (((1,), (1,)), ((), ())), preferred...  6.67 us
  transfers between devices with their start and end apart: 8, of which 8 were waited for; matrix products, arithmetic and copies ran while one was open for 25% of the time, Pallas kernels for 0%

commit v1 on v0

v1 whole, which is shorter than its diff:
```python
import jax
import jax.numpy as jnp
from jax import lax
from jax.experimental import pallas as pl
from jax.experimental.pallas import tpu as pltpu
from jax.sharding import PartitionSpec as P

MESH = pl.DeviceIdType.MESH
NY, NZ, NX, NCTX = 4, 8, 4, 8
SEG = 8
LANES = 128


def kernel(
    g_hbm, w_hbm, q_hbm, v_hbm, r_ref, a_ref,
    gq_hbm, gi_hbm,
    gbuf, wbuf, pbuf, hbuf, rbuf, qbuf, vbuf, gc, yf, gqb, gib,
    ab, rb, m1, m2, m4, a7, bpow, sown, sall,
    lsem, asend, arecv, gsend, grecv, xsend, xrecv, ysend, yrecv, ssend, srecv,
):
    f32 = jnp.float32
    ctx = lax.axis_index("ctx")
    ch = lax.axis_index("ch")
    y = ch // NZ
    z = ch % NZ
    tok = gq_hbm.shape[0]
    wid = gq_hbm.shape[1]
    modes = a_ref.shape[0]
    steps = tok // SEG

    def at_z(d):
        return (ctx, y * NZ + (z + d + NZ) % NZ)

    def at_y(d):
        return (ctx, ((y + d + NY) % NY) * NZ + z)

    def at_ctx(d):
        return ((ctx + d + NCTX) % NCTX, ch)

    twin = ctx + 1 - 2 * (ctx % 2)
    at_twin = (twin, ch)

    locals_ = [
        pltpu.make_async_copy(g_hbm, gbuf.at[0], lsem.at[0]),
        pltpu.make_async_copy(q_hbm, qbuf, lsem.at[1]),
        pltpu.make_async_copy(v_hbm, vbuf, lsem.at[2]),
    ]
    for dy in range(NY):
        first = (((y + dy) % NY) * NZ + z) * NCTX
        locals_.append(
            pltpu.make_async_copy(w_hbm.at[pl.ds(first, NCTX)], wbuf.at[dy, :, 0], lsem.at[3 + dy])
        )
    for c in locals_:
        c.start()

    barrier = pltpu.get_barrier_semaphore()
    peers = [at_z(d) for d in range(1, NZ)] + [at_y(1), at_y(-1)]
    peers += [at_ctx(d) for d in range(1, NCTX)]
    for p in peers:
        pl.semaphore_signal(barrier, inc=1, device_id=p, device_id_type=MESH)
    pl.semaphore_wait(barrier, len(peers))

    def rcopy(src, dst, ssem, rsem, dev):
        return pltpu.make_async_remote_copy(
            src_ref=src, dst_ref=dst, send_sem=ssem, recv_sem=rsem, device_id=dev, device_id_type=MESH
        )

    def spread(dy):
        for o in range(1, NZ):
            zz = (z - o + NZ) % NZ
            row = (((y + dy) % NY) * NZ + zz) * NCTX + ctx
            rcopy(w_hbm.at[row], wbuf.at[dy, ctx, o], asend.at[dy], arecv.at[dy], at_z(-o)).start()

    def block(dy, who, lo, n):
        return wbuf.at[dy, who, pl.ds(lo, n)]

    full = (1, NZ - 1)
    part_a = (1, 4)
    part_b = (5, 3)
    back = (ctx + NCTX - 2) % NCTX
    ahead = (ctx + 2) % NCTX
    far = (ctx + 4) % NCTX
    links = {
        0: (ctx, full, at_ctx(2)),
        1: (ctx, full, at_ctx(-2)),
        2: (back, part_a, at_ctx(2)),
        3: (ahead, part_b, at_ctx(-2)),
        4: (ctx, full, at_twin),
        5: (back, full, at_twin),
        6: (ahead, full, at_twin),
        7: (far, part_a, at_twin),
        8: (far, part_b, at_twin),
    }
    tback = (twin + NCTX - 2) % NCTX
    tahead = (twin + 2) % NCTX
    tfar = (twin + 4) % NCTX
    lands = {
        0: (back, full), 1: (ahead, full), 2: (far, part_a), 3: (far, part_b),
        4: (twin, full), 5: (tback, full), 6: (tahead, full), 7: (tfar, part_a), 8: (tfar, part_b),
    }

    def xcopy(dy, k):
        who, part, dev = links[k]
        ref = block(dy, who, *part)
        return rcopy(ref, ref, xsend.at[dy, k], xrecv.at[dy, k], dev)

    def xwait(dy, k):
        who, part = lands[k]
        ref = block(dy, who, *part)
        rcopy(ref, ref, xsend.at[dy, k], xrecv.at[dy, k], at_twin).wait_recv()

    def share0(dy):
        ref = block(dy, ctx, *full)
        rcopy(ref, ref, asend.at[dy], arecv.at[dy], at_twin).wait_recv()
        for k in (0, 1, 4):
            xcopy(dy, k).start()

    def share1(dy):
        xwait(dy, 0)
        xcopy(dy, 2).start()
        xcopy(dy, 5).start()
        xwait(dy, 1)
        xcopy(dy, 3).start()
        xcopy(dy, 6).start()

    def share2(dy):
        xwait(dy, 2)
        xcopy(dy, 7).start()
        xwait(dy, 3)
        xcopy(dy, 8).start()

    def share3(dy):
        for k in (4, 5, 6, 7, 8):
            xwait(dy, k)

    half = tok // 2
    lo_rows = pl.ds(0, half)
    hi_rows = pl.ds(half, half)

    def gcopy(k):
        if k < 3:
            src, dst, dev = (0, NZ - 1, 1) if k == 0 else (NZ - k, NZ - k - 1, 1)
        elif k == 3:
            return rcopy(gbuf.at[5, lo_rows], gbuf.at[4, lo_rows], gsend.at[3], grecv.at[3], at_z(1))
        elif k < 7:
            src, dst, dev = k - 4, k - 3, -1
        else:
            return rcopy(gbuf.at[3, hi_rows], gbuf.at[4, hi_rows], gsend.at[7], grecv.at[7], at_z(-1))
        source = g_hbm if src == 0 else gbuf.at[src]
        return rcopy(source, gbuf.at[dst], gsend.at[k], grecv.at[k], at_z(dev))

    def gather0():
        gcopy(0).start()
        gcopy(4).start()

    def gather(h):
        gcopy(h - 1).wait_recv()
        gcopy(h).start()
        gcopy(h + 3).wait_recv()
        gcopy(h + 4).start()

    def gather_done():
        gcopy(3).wait_recv()
        gcopy(7).wait_recv()

    spread(2)
    spread(1)
    gather0()

    a_t = a_ref[...]
    r_t = r_ref[...]
    seg = lax.broadcasted_iota(jnp.int32, (SEG, wid), 0)
    for n in range(modes):
        a1 = jnp.broadcast_to(a_t[n : n + 1], (SEG, wid))
        ab[n] = a1
        rb[n] = jnp.broadcast_to(r_t[n : n + 1], (SEG, wid))
        p = a1
        for _ in range(5):
            p = p * p
        p2 = p * p
        p4 = p2 * p2
        m1[n] = jnp.where(seg < SEG - 1, p, 0.0)
        m2[n] = jnp.where(seg < SEG - 2, p2, 0.0)
        m4[n] = jnp.where(seg < SEG - 4, p4, 0.0)
        left = SEG - 1 - seg
        a7[n] = (
            jnp.where(left % 2 == 1, p, 1.0)
            * jnp.where((left // 2) % 2 == 1, p2, 1.0)
            * jnp.where(left // 4 == 1, p4, 1.0)
        )
    b = a_t
    for _ in range(8):
        b = b * b
    bpow[...] = b

    def partial(dy):
        g = jnp.concatenate([gbuf[o] for o in range(NZ)], axis=1)
        w = jnp.concatenate([wbuf[dy, :, o].reshape(wid, wid) for o in range(NZ)], axis=1)
        return lax.dot_general(g, w, (((1,), (1,)), ((), ())), preferred_element_type=f32)

    share0(2)
    gather(1)
    share0(1)
    share1(2)
    gather(2)
    spread(3)
    share1(1)
    share2(2)
    gather(3)
    spread(0)
    share2(1)
    share3(2)
    for c in locals_:
        c.wait()
    gather_done()

    pbuf[2] = partial(2)
    far0 = rcopy(pbuf.at[2, lo_rows], hbuf.at[0], ysend.at[0], yrecv.at[0], at_y(1))
    far1 = rcopy(pbuf.at[2, hi_rows], hbuf.at[1], ysend.at[1], yrecv.at[1], at_y(-1))
    far0.start()
    far1.start()
    share0(3)
    share3(1)
    pbuf[1] = partial(1)
    share1(3)
    share0(0)
    far0.wait_recv()
    pbuf[1, lo_rows] += hbuf[0]
    near0 = rcopy(pbuf.at[1], rbuf.at[0], ysend.at[2], yrecv.at[2], at_y(1))
    near0.start()
    share2(3)
    share1(0)
    share3(3)
    pbuf[3] = partial(3)
    far1.wait_recv()
    pbuf[3, hi_rows] += hbuf[1]
    near1 = rcopy(pbuf.at[3], rbuf.at[1], ysend.at[3], yrecv.at[3], at_y(-1))
    near1.start()
    share2(0)
    share3(0)
    pbuf[0] = partial(0)
    near0.wait_recv()
    near1.wait_recv()

    mix = pbuf[0] + rbuf[0] + rbuf[1]
    conv = mix * qbuf[...].astype(f32)
    for col in range(0, wid, LANES):
        gc[col // LANES] = conv[:, col : col + LANES]
    gqb[...] = (mix * vbuf[...].astype(f32)).astype(jnp.bfloat16)
    out_q = pltpu.make_async_copy(gqb, gq_hbm, lsem.at[7])
    out_q.start()

    lanes = LANES
    unroll = 8

    def sweep(j, state, poles, col):
        row = gc[col // lanes, pl.ds(j, SEG, stride=steps)]
        return [poles[n] * state[n] + row for n in range(modes)]

    ends = []
    for col in range(0, wid, lanes):
        cols = slice(col, col + lanes)
        poles = [ab[n, :, cols] for n in range(modes)]

        def first(k, state, poles=poles, col=col):
            state = list(state)
            for u in range(unroll):
                state = sweep(steps - 1 - (k * unroll + u), state, poles, col)
            return tuple(state)

        zero = tuple(jnp.zeros((SEG, lanes), f32) for _ in range(modes))
        state = lax.fori_loop(0, steps // unroll, first, zero)
        for n in range(modes):
            s = state[n]
            s = s + m1[n, :, cols] * pltpu.roll(s, SEG - 1, 0)
            s = s + m2[n, :, cols] * pltpu.roll(s, SEG - 2, 0)
            s = s + m4[n, :, cols] * pltpu.roll(s, SEG - 4, 0)
            sown[pl.ds(n, 1), cols] = s[0:1]
            ends.append(jnp.where(seg[:, :lanes] < SEG - 1, pltpu.roll(s, SEG - 1, 0), 0.0))
    for t in range(len(ends)):
        col = (t // modes) * lanes
        m1[t % modes, :, col : col + lanes] = ends[t]

    states = [
        rcopy(sown, sall.at[NCTX - d], ssend.at[d], srecv.at[NCTX - d], at_ctx(d))
        for d in range(1, NCTX)
    ]
    for s in states:
        s.start()
    incoming = jnp.zeros((modes, wid), f32)
    for d in range(NCTX - 1, 0, -1):
        rcopy(sown, sall.at[d], ssend.at[d], srecv.at[d], at_ctx(d)).wait_recv()
        here = jnp.where(ctx + d < NCTX, 1.0, 0.0).astype(f32)
        incoming = bpow[...] * incoming + here * sall[d]

    for col in range(0, wid, lanes):
        cols = slice(col, col + lanes)
        poles = [ab[n, :, cols] for n in range(modes)]
        gains = [rb[n, :, cols] for n in range(modes)]
        state = tuple(
            m1[n, :, cols] + a7[n, :, cols] * incoming[n : n + 1, cols] for n in range(modes)
        )

        def second(k, state, poles=poles, gains=gains, col=col):
            state = list(state)
            for u in range(unroll):
                j = steps - 1 - (k * unroll + u)
                state = sweep(j, state, poles, col)
                terms = [gains[n] * state[n] for n in range(modes)]
                while len(terms) > 1:
                    terms = [terms[m] + terms[m + 1] for m in range(0, len(terms), 2)]
                yf[col // lanes, pl.ds(j, SEG, stride=steps)] = terms[0]
            return tuple(state)

        lax.fori_loop(0, steps // unroll, second, state)
    for col in range(0, wid, lanes):
        gib[:, col : col + lanes] = yf[col // lanes].astype(jnp.bfloat16)
    out_i = pltpu.make_async_copy(gib, gi_hbm, lsem.at[8])
    out_i.start()

    for dy in range(NY):
        ref = block(dy, ctx, *full)
        rcopy(ref, ref, asend.at[dy], arecv.at[dy], at_twin).wait_send()
        for k in range(9):
            xcopy(dy, k).wait_send()
    for k in range(8):
        gcopy(k).wait_send()
    for c in (far0, far1, near0, near1):
        c.wait_send()
    for s in states:
        s.wait_send()
    out_q.wait()
    out_i.wait()


def local(out_grad, out_weight, query_in, conv_out, residues, decay_rates):
    tok, wid = query_in.shape
    modes = residues.shape[1]
    bf16, f32 = jnp.bfloat16, jnp.float32
    chunk = wid // NCTX
    w = out_weight.reshape(out_weight.shape[0] // chunk, chunk, out_weight.shape[1])
    any_ = pl.BlockSpec(memory_space=pl.ANY)
    vm = pl.BlockSpec(memory_space=pltpu.VMEM)
    dma = pltpu.SemaphoreType.DMA
    table = pltpu.VMEM((modes, SEG, wid), f32)
    return pl.pallas_call(
        kernel,
        out_shape=(
            jax.ShapeDtypeStruct((tok, wid), bf16),
            jax.ShapeDtypeStruct((tok, wid), bf16),
        ),
        in_specs=[any_, any_, any_, any_, vm, vm],
        out_specs=(any_, any_),
        scratch_shapes=[
            pltpu.VMEM((NZ, tok, wid), bf16),
            pltpu.VMEM((NY, NCTX, NZ, chunk, wid), bf16),
            pltpu.VMEM((NY, tok, wid), f32),
            pltpu.VMEM((2, tok // 2, wid), f32),
            pltpu.VMEM((2, tok, wid), f32),
            pltpu.VMEM((tok, wid), bf16),
            pltpu.VMEM((tok, wid), bf16),
            pltpu.VMEM((wid // LANES, tok, LANES), f32),
            pltpu.VMEM((wid // LANES, tok, LANES), f32),
            pltpu.VMEM((tok, wid), bf16),
            pltpu.VMEM((tok, wid), bf16),
            table, table, table, table, table, table,
            pltpu.VMEM((modes, wid), f32),
            pltpu.VMEM((modes, wid), f32),
            pltpu.VMEM((NCTX, modes, wid), f32),
            dma((9,)),
            dma((NY,)), dma((NY,)),
            dma((8,)), dma((8,)),
            dma((NY, 9)), dma((NY, 9)),
            dma((4,)), dma((4,)),
            dma((NCTX,)), dma((NCTX,)),
        ],
        compiler_params=pltpu.CompilerParams(
            collective_id=0, has_side_effects=True
        ),
        name="mix_and_scan",
    )(out_grad, w, query_in, conv_out, residues.T, decay_rates.T)


def solution(mesh):
    placed = (
        P("ctx", "ch"),
        P(None, "ch"),
        P("ctx", "ch"),
        P("ctx", "ch"),
        P("ch", None),
        P("ch", None),
    )
    return jax.shard_map(
        local,
        mesh=mesh,
        in_specs=placed,
        out_specs=(P("ctx", "ch"), P("ctx", "ch")),
        check_vma=False,
    )
```

time: 329 us -> 65.5 us (0.20)
  waiting for transfers between devices: 167 us -> 0 us
  local copies, waits for them, and re-layouts: 84.3 us -> 3.14 us
  Pallas kernels: 0 us -> 61.4 us
  matrix products: 41.8 us -> 0 us
  starting transfers between devices: 18 us -> 0 us
  between operations: 14.2 us -> 0.64 us
    reduce_scatter x1 -> x0, waiting for transfers between devices: 146 us -> none  [local(): lax.psum_scatter(lax.dot_general(out_weight, out_grad, (((1,), (1,)), (()...]
    gather x2 -> x0, local copies, waits for them, and re-layouts: 80.2 us -> none  [local(): jnp.take(filter_taps, jnp.maximum(lagged, 0), axis=0)]
    pallas_call x0 -> x1, Pallas kernels: none -> 61.4 us  [local(): pl.pallas_call(kernel, out_shape=(jax.ShapeDtypeStruct((tok, wid), bf16),...]
    dot_general x4 -> x0, matrix products: 41.8 us -> none  [the longest x1 28.7 us: local(): inner_part = jnp.einsum('stc,btc->bsc', toeplitz, blocks, precision=highest)]
    ppermute x7 -> x0, waiting for transfers between devices: 21.2 us -> none  [from_behind(): return lax.ppermute(shard, axis, pairs)]
    ppermute x7 -> x0, starting transfers between devices: 17.9 us -> none  [from_behind(): return lax.ppermute(shard, axis, pairs)]
  transfers between devices with their start and end apart: 8 -> 0, of which waited for: 8 -> 0; matrix products, arithmetic and copies ran while one was open for 25% -> 0% of each run, Pallas kernels for 0% -> 0%
where the time goes in v1:
time: 65.5 us; the launch traced here: 65.2 us
  Pallas kernels  61.4 us (94%)
  local copies, waits for them, and re-layouts  3.14 us (5%)
    pallas_call x1, Pallas kernels, local(): pl.pallas_call(kernel, out_shape=(jax.ShapeDtypeStruct((tok, wid), bf16),...  61.4 us
    unnamed x2, local copies, waits for them, and re-layouts  3.14 us

profile of v1, /device:TPU:1, one launch (start us, length us, event | category | flops | bytes accessed | tf_op | source)
XLA Modules:
  0.0 65.2 jit_solution(13008021454019756577)
XLA Ops:
  0.6 61.4 %mix_and_scan.1 = (bf16[256,256]{1,0:T(8,128)(2,1)}, bf16[256,256]{1,0:T(8,128)(2,1)}) custom-call(bf16[256,256]{1,0:T(8,128)(2,1)} %g_hbm.1, bf16[256,32,256]{2,1,0:T(8,128)(2,1)} %bitcast.3, bf16[256,256]{1,0:T(8,128)(2,1)} %q_hbm.1, bf16[256,256]{1,0:T(8,128)(2,1)} %v_hbm.1, f32[16,256]{1,0:T(8,128)} %bitcast.4, f32[16,256]{1,0:T(8,128)} %bitcast.5), custom_call_target="tpu_custom_call" | custom-call | tf_op jit(solution)/shard_map/mix_and_scan/pallas_call | solution.py:346
  62.1 1.6 %copy.10 = bf16[256,256]{1,0:T(8,128)(2,1)} copy(bf16[256,256]{1,0:T(8,128)(2,1)} %get-tuple-element.4) | data formatting | bytes 262144
  63.6 1.6 %copy.11 = bf16[256,256]{1,0:T(8,128)(2,1)} copy(bf16[256,256]{1,0:T(8,128)(2,1)} %get-tuple-element.5) | data formatting | bytes 262144

commit v2 on v1

v2 whole, which is shorter than its diff:
```python
import jax
import jax.numpy as jnp
from jax import lax
from jax.experimental import pallas as pl
from jax.experimental.pallas import tpu as pltpu
from jax.sharding import PartitionSpec as P

MESH = pl.DeviceIdType.MESH
NY, NZ, NX, NCTX = 4, 8, 4, 8
SEG = 8
LANES = 128
UNROLL = 8
NH = 2
FIRST = ((0, 2), (0, 1), (0, 3), (1, 0), (1, 1))
ARRIVED, SHARED, GATHERED, SUMMED, ADDED, SPREAD = range(6)
EVENTS = (
    (0, 2, 0), (1, 2, 2), (0, 1, 0), (1, 2, 0), (1, 2, 1), (1, 2, 3), (2, 0, 0), (5, 0, 0), (2, 0, 4),
    (1, 2, 5), (0, 3, 0), (1, 1, 0), (1, 1, 2), (2, 1, 0), (2, 1, 4), (1, 1, 1), (1, 1, 3), (1, 2, 4),
    (2, 0, 1), (1, 3, 2), (1, 3, 0), (1, 3, 3), (1, 3, 1), (2, 0, 5), (1, 1, 5), (1, 1, 4), (1, 3, 5),
    (2, 1, 1), (2, 1, 5), (0, 0, 0), (1, 3, 4), (2, 0, 2), (2, 0, 6), (1, 0, 2), (2, 1, 2), (2, 1, 6),
    (1, 0, 0), (1, 0, 1), (1, 0, 3), (2, 0, 3), (3, 2, 0), (3, 1, 0), (3, 3, 0), (1, 0, 5), (2, 1, 7),
    (3, 2, 1), (3, 1, 1), (3, 3, 1), (1, 0, 4), (3, 0, 0), (3, 0, 1), (4, 0, 0), (4, 0, 1), (4, 1, 0),
    (4, 1, 1),
)


def sweep(gc, j, state, poles, col):
    row = gc[col // LANES, pl.ds(j, SEG, stride=gc.shape[1] // SEG)]
    return [p * s + row for p, s in zip(poles, state)]


def kernel(
    g_hbm, w_hbm, q_hbm, v_hbm, r_hbm, a_hbm,
    gqb, gc, ab, rb, start,
    gbuf, wbuf, pbuf, hbuf, rbuf, qbuf, vbuf, r_ref, a_ref,
    m1, m2, m4, a7, bpow, sown, sall,
    lsem, asend, arecv, gsend, grecv, xsend, xrecv, ysend, yrecv, ssend, srecv,
):
    f32 = jnp.float32
    ctx = lax.axis_index("ctx")
    ch = lax.axis_index("ch")
    y = ch // NZ
    z = ch % NZ
    tok, wid = q_hbm.shape
    modes = a_hbm.shape[0]
    steps = tok // SEG

    def at_z(d):
        return (ctx, y * NZ + (z + d + NZ) % NZ)

    def at_y(d):
        return (ctx, ((y + d + NY) % NY) * NZ + z)

    def at_ctx(d):
        return ((ctx + d + NCTX) % NCTX, ch)

    twin = ctx + 1 - 2 * (ctx % 2)
    at_twin = (twin, ch)

    locals_ = [
        pltpu.make_async_copy(g_hbm, gbuf.at[0], lsem.at[0]),
        pltpu.make_async_copy(q_hbm, qbuf, lsem.at[1]),
        pltpu.make_async_copy(v_hbm, vbuf, lsem.at[2]),
    ]
    for dy in range(NY):
        first = (((y + dy) % NY) * NZ + z) * NCTX
        locals_.append(
            pltpu.make_async_copy(w_hbm.at[pl.ds(first, NCTX)], wbuf.at[dy, :, 0], lsem.at[3 + dy])
        )
    poles_in = [
        pltpu.make_async_copy(r_hbm, r_ref, lsem.at[7]),
        pltpu.make_async_copy(a_hbm, a_ref, lsem.at[8]),
    ]
    for c in locals_ + poles_in:
        c.start()

    barrier = pltpu.get_barrier_semaphore()
    peers = [at_z(d) for d in range(1, NZ)] + [at_y(1), at_y(-1)]
    peers += [at_ctx(d) for d in range(1, NCTX)]
    for p in peers:
        pl.semaphore_signal(barrier, inc=1, device_id=p, device_id_type=MESH)
    pl.semaphore_wait(barrier, len(peers))

    def rcopy(src, dst, ssem, rsem, dev):
        return pltpu.make_async_remote_copy(
            src_ref=src, dst_ref=dst, send_sem=ssem, recv_sem=rsem, device_id=dev, device_id_type=MESH
        )

    def spread(dy):
        for o in range(1, NZ):
            zz = (z - o + NZ) % NZ
            row = (((y + dy) % NY) * NZ + zz) * NCTX + ctx
            rcopy(w_hbm.at[row], wbuf.at[dy, ctx, o], asend.at[dy], arecv.at[dy], at_z(-o)).start()

    def block(dy, who, lo, n):
        return wbuf.at[dy, who, pl.ds(lo, n)]

    full = (1, NZ - 1)
    part_a = (1, 4)
    part_b = (5, 3)

    def beside(who):
        return (who + NCTX - 2) % NCTX, (who + 2) % NCTX, (who + 4) % NCTX

    back, ahead, far_off = beside(ctx)
    up, down = at_ctx(2), at_ctx(-2)
    links = (
        (ctx, part_a, up), (ctx, part_b, up), (ctx, part_b, down), (ctx, part_a, down),
        (back, part_a, up), (ahead, part_b, down),
        (ctx, full, at_twin), (back, part_a, at_twin), (back, part_b, at_twin), (ahead, part_b, at_twin),
        (ahead, part_a, at_twin), (far_off, part_a, at_twin), (far_off, part_b, at_twin),
    )
    tback, tahead, tfar = beside(twin)
    lands = (
        (back, part_a), (back, part_b), (ahead, part_b), (ahead, part_a),
        (far_off, part_a), (far_off, part_b),
        (twin, full), (tback, part_a), (tback, part_b), (tahead, part_b),
        (tahead, part_a), (tfar, part_a), (tfar, part_b),
    )

    def xcopy(dy, k):
        who, part, dev = links[k]
        ref = block(dy, who, *part)
        return rcopy(ref, ref, xsend.at[dy, k], xrecv.at[dy, k], dev)

    def xwait(dy, k):
        who, part = lands[k]
        ref = block(dy, who, *part)
        rcopy(ref, ref, xsend.at[dy, k], xrecv.at[dy, k], at_twin).wait_recv()

    def arrived(dy):
        ref = block(dy, ctx, *full)
        rcopy(ref, ref, asend.at[dy], arecv.at[dy], at_twin).wait_recv()
        for k in (0, 2, 1, 3, 6):
            xcopy(dy, k).start()

    def shared(dy, k):
        xwait(dy, k)
        if k == 0:
            xcopy(dy, 4).start()
        if k == 2:
            xcopy(dy, 5).start()
        xcopy(dy, 7 + k).start()

    half = tok // NH
    quarter = half // 2

    def rows(h):
        return pl.ds(h * half, half)

    def gcopy(h, k):
        up = k < 4
        hop = k % 4
        src = (NZ - hop) % NZ if up else hop
        dst = NZ - hop - 1 if up else hop + 1
        source = g_hbm if hop == 0 else gbuf.at[src]
        return rcopy(
            source.at[rows(h)], gbuf.at[dst, rows(h)], gsend.at[h, k], grecv.at[h, k], at_z(1 if up else -1)
        )

    def last(h):
        return 3 if h < NH // 2 else 7

    def gather0(h):
        gcopy(h, 0).start()
        gcopy(h, 4).start()

    def gathered(h, k):
        gcopy(h, k).wait_recv()
        if k % 4 < 2 or k + 1 == last(h):
            gcopy(h, k + 1).start()

    for kind, n in FIRST:
        gather0(n) if kind else spread(n)

    for c in poles_in:
        c.wait()
    a_t = a_ref[...]
    r_t = r_ref[...]
    seg = lax.broadcasted_iota(jnp.int32, (SEG, wid), 0)
    for n in range(modes):
        a1 = jnp.broadcast_to(a_t[n : n + 1], (SEG, wid))
        ab[n] = a1
        rb[n] = jnp.broadcast_to(r_t[n : n + 1], (SEG, wid))
        p = a1
        for _ in range(5):
            p = p * p
        p2 = p * p
        p4 = p2 * p2
        m1[n] = jnp.where(seg < SEG - 1, p, 0.0)
        m2[n] = jnp.where(seg < SEG - 2, p2, 0.0)
        m4[n] = jnp.where(seg < SEG - 4, p4, 0.0)
        left = SEG - 1 - seg
        a7[n] = (
            jnp.where(left % 2 == 1, p, 1.0)
            * jnp.where((left // 2) % 2 == 1, p2, 1.0)
            * jnp.where(left // 4 == 1, p4, 1.0)
        )
    b = a_t
    for _ in range(8):
        b = b * b
    bpow[...] = b

    def partial(dy, h):
        g = jnp.concatenate([gbuf[o, rows(h)] for o in range(NZ)], axis=1)
        w = jnp.concatenate([wbuf[dy, :, o].reshape(wid, wid) for o in range(NZ)], axis=1)
        pbuf[dy, rows(h)] = lax.dot_general(
            g, w, (((1,), (1,)), ((), ())), preferred_element_type=f32
        )

    def quart(h, side):
        return pl.ds(h * half + side * quarter, quarter)

    def far(h, side):
        return rcopy(
            pbuf.at[2, quart(h, side)], hbuf.at[side, h],
            ysend.at[0, side, h], yrecv.at[0, side, h], at_y(1 - 2 * side),
        )

    def near(h, side, late):
        part = quart(h, side if late else 1 - side)
        return rcopy(
            pbuf.at[1 + 2 * side, part], rbuf.at[side, part],
            ysend.at[1 + late, side, h], yrecv.at[1 + late, side, h], at_y(1 - 2 * side),
        )

    def summed(dy, h):
        partial(dy, h)
        if dy == 2:
            far(h, 0).start()
            far(h, 1).start()
        elif dy:
            near(h, dy // 2, 0).start()

    def added(h, side):
        far(h, side).wait_recv()
        pbuf[1 + 2 * side, quart(h, side)] += hbuf[side, h]
        near(h, side, 1).start()

    here = False
    whole = set()
    for what, a, b in EVENTS:
        if what == ARRIVED:
            arrived(a)
        elif what == SHARED:
            shared(a, b)
        elif what == GATHERED:
            gathered(a, b)
        elif what == ADDED:
            added(a, b)
        elif what == SPREAD:
            spread(a)
        else:
            if not here:
                for c in locals_:
                    c.wait()
                here = True
            if a not in whole:
                whole.add(a)
                for k in range(6, 13):
                    xwait(a, k)
            summed(a, b)
    for h in range(NH):
        for side in range(2):
            near(h, side, 0).wait_recv()
            near(h, side, 1).wait_recv()

    mix = pbuf[0] + rbuf[0] + rbuf[1]
    conv = mix * qbuf[...].astype(f32)
    for col in range(0, wid, LANES):
        gc[col // LANES] = conv[:, col : col + LANES]
    gqb[...] = (mix * vbuf[...].astype(f32)).astype(jnp.bfloat16)
    lanes = LANES

    ends = []
    for col in range(0, wid, lanes):
        cols = slice(col, col + lanes)
        poles = [ab[n, :, cols] for n in range(modes)]

        def first(k, state, poles=poles, col=col):
            state = list(state)
            for u in range(UNROLL):
                state = sweep(gc, steps - 1 - (k * UNROLL + u), state, poles, col)
            return tuple(state)

        zero = tuple(jnp.zeros((SEG, lanes), f32) for _ in range(modes))
        state = lax.fori_loop(0, steps // UNROLL, first, zero)
        for n in range(modes):
            s = state[n]
            s = s + m1[n, :, cols] * pltpu.roll(s, SEG - 1, 0)
            s = s + m2[n, :, cols] * pltpu.roll(s, SEG - 2, 0)
            s = s + m4[n, :, cols] * pltpu.roll(s, SEG - 4, 0)
            sown[pl.ds(n, 1), cols] = s[0:1]
            ends.append(jnp.where(seg[:, :lanes] < SEG - 1, pltpu.roll(s, SEG - 1, 0), 0.0))
    states = [
        rcopy(sown, sall.at[NCTX - d], ssend.at[d], srecv.at[NCTX - d], at_ctx(d))
        for d in range(1, NCTX)
    ]
    for s in states:
        s.start()
    incoming = jnp.zeros((modes, wid), f32)
    for d in range(NCTX - 1, 0, -1):
        rcopy(sown, sall.at[d], ssend.at[d], srecv.at[d], at_ctx(d)).wait_recv()
        here = jnp.where(ctx + d < NCTX, 1.0, 0.0).astype(f32)
        incoming = bpow[...] * incoming + here * sall[d]

    for t in range(len(ends)):
        n, col = t % modes, (t // modes) * lanes
        cols = slice(col, col + lanes)
        start[n, :, cols] = ends[t] + a7[n, :, cols] * incoming[n : n + 1, cols]

    for dy in range(NY):
        ref = block(dy, ctx, *full)
        rcopy(ref, ref, asend.at[dy], arecv.at[dy], at_twin).wait_send()
        for k in range(13):
            xcopy(dy, k).wait_send()
    for k in range(8):
        for h in range(NH):
            if k % 4 < 3 or k == last(h):
                gcopy(h, k).wait_send()
    for h in range(NH):
        for side in range(2):
            far(h, side).wait_send()
            near(h, side, 0).wait_send()
            near(h, side, 1).wait_send()
    for s in states:
        s.wait_send()


def finish(gqb, gc, ab, rb, start, gq_hbm, gi_hbm, yf, gib, sem):
    modes, _, wid = ab.shape
    steps = gqb.shape[0] // SEG
    out_q = pltpu.make_async_copy(gqb, gq_hbm, sem.at[0])
    out_q.start()
    for col in range(0, wid, LANES):
        cols = slice(col, col + LANES)
        poles = [ab[n, :, cols] for n in range(modes)]
        gains = [rb[n, :, cols] for n in range(modes)]

        def second(k, state, poles=poles, gains=gains, col=col):
            state = list(state)
            for u in range(UNROLL):
                j = steps - 1 - (k * UNROLL + u)
                state = sweep(gc, j, state, poles, col)
                terms = [gains[n] * state[n] for n in range(modes)]
                while len(terms) > 1:
                    terms = [terms[m] + terms[m + 1] for m in range(0, len(terms), 2)]
                yf[col // LANES, pl.ds(j, SEG, stride=steps)] = terms[0]
            return tuple(state)

        lax.fori_loop(0, steps // UNROLL, second, tuple(start[n, :, cols] for n in range(modes)))
        gib[:, cols] = yf[col // LANES].astype(gib.dtype)
    out_i = pltpu.make_async_copy(gib, gi_hbm, sem.at[1])
    out_i.start()
    out_q.wait()
    out_i.wait()


def local(out_grad, out_weight, query_in, conv_out, residues, decay_rates):
    tok, wid = query_in.shape
    modes = residues.shape[1]
    bf16, f32 = jnp.bfloat16, jnp.float32
    chunk = wid // NCTX
    w = out_weight.reshape(out_weight.shape[0] // chunk, chunk, out_weight.shape[1])
    any_ = pl.BlockSpec(memory_space=pltpu.HBM)
    vm = pl.BlockSpec(memory_space=pltpu.VMEM)
    dma = pltpu.SemaphoreType.DMA
    table = pltpu.VMEM((modes, SEG, wid), f32)
    full = jax.ShapeDtypeStruct((tok, wid), bf16)
    tall = jax.ShapeDtypeStruct((modes, SEG, wid), f32)
    inputs = (out_grad, w, query_in, conv_out, residues.T, decay_rates.T)
    held = pl.pallas_call(
        kernel,
        out_shape=(full, jax.ShapeDtypeStruct((wid // LANES, tok, LANES), f32), tall, tall, tall),
        in_specs=[any_] * 6,
        out_specs=(vm,) * 5,
        scratch_shapes=[
            pltpu.VMEM((NZ, tok, wid), bf16),
            pltpu.VMEM((NY, NCTX, NZ, chunk, wid), bf16),
            pltpu.VMEM((NY, tok, wid), f32),
            pltpu.VMEM((2, NH, tok // NH // 2, wid), f32),
            pltpu.VMEM((2, tok, wid), f32),
            pltpu.VMEM((tok, wid), bf16),
            pltpu.VMEM((tok, wid), bf16),
            pltpu.VMEM((modes, wid), f32),
            pltpu.VMEM((modes, wid), f32),
            table, table, table, table,
            pltpu.VMEM((modes, wid), f32),
            pltpu.VMEM((modes, wid), f32),
            pltpu.VMEM((NCTX, modes, wid), f32),
            dma((9,)),
            dma((NY,)), dma((NY,)),
            dma((NH, 8)), dma((NH, 8)),
            dma((NY, 13)), dma((NY, 13)),
            dma((3, 2, NH)), dma((3, 2, NH)),
            dma((NCTX,)), dma((NCTX,)),
        ],
        compiler_params=pltpu.CompilerParams(
            collective_id=0, has_side_effects=True, vmem_limit_bytes=55_000_000
        ),
        name="mix",
    )(*[pltpu.with_memory_space_constraint(t, pltpu.HBM) for t in inputs])
    return pl.pallas_call(
        finish,
        out_shape=(full, full),
        in_specs=[vm] * 5,
        out_specs=(any_, any_),
        scratch_shapes=[
            pltpu.VMEM((wid // LANES, tok, LANES), f32),
            pltpu.VMEM((tok, wid), bf16),
            dma((2,)),
        ],
        compiler_params=pltpu.CompilerParams(vmem_limit_bytes=16 * 1024 * 1024),
        name="finish",
    )(*held)


def solution(mesh):
    placed = (
        P("ctx", "ch"),
        P(None, "ch"),
        P("ctx", "ch"),
        P("ctx", "ch"),
        P("ch", None),
        P("ch", None),
    )
    return jax.shard_map(
        local,
        mesh=mesh,
        in_specs=placed,
        out_specs=(P("ctx", "ch"), P("ctx", "ch")),
        check_vma=False,
    )
```

time: 65.5 us -> 56.7 us (0.87)
  Pallas kernels: 61.4 us -> 56 us
  local copies, waits for them, and re-layouts: 3.14 us -> 0 us
    pallas_call x1 -> x2, Pallas kernels: 61.4 us -> 56 us  [the longest x1 54.4 us: local(): pl.pallas_call(kernel, out_shape=(full, jax.ShapeDtypeStruct((wid // LANE...]
    unnamed x2 -> x0, local copies, waits for them, and re-layouts: 3.14 us -> none
where the time goes in v2:
time: 56.7 us; the launch traced here: 56.6 us
  Pallas kernels  56 us (99%)
  between operations  0.64 us (1%)
    pallas_call x1, Pallas kernels, local(): pl.pallas_call(kernel, out_shape=(full, jax.ShapeDtypeStruct((wid // LANE...  54.4 us
    pallas_call x1, Pallas kernels, local(): pl.pallas_call(finish, out_shape=(full, full), in_specs=[vm] * 5, out_spe...  1.58 us

profile of v2, /device:TPU:1, one launch (start us, length us, event | category | flops | bytes accessed | tf_op | source)
XLA Modules:
  0.0 56.6 jit_solution(7568434094984806298)
XLA Ops:
  0.6 54.4 %mix.1 = (bf16[256,256]{1,0:T(8,128)(2,1)S(1)}, f32[2,256,128]{2,1,0:T(8,128)S(1)}, f32[16,8,256]{2,1,0:T(8,128)S(1)}, f32[16,8,256]{2,1,0:T(8,128)S(1)}, f32[16,8,256]{2,1,0:T(8,128)S(1)}) custom-call(bf16[256,256]{1,0:T(8,128)(2,1)} %g_hbm.1, bf16[256,32,256]{2,1,0:T(8,128)(2,1)} %bitcast.3, bf16[256,256]{1,0:T(8,128)(2,1)} %q_hbm.1, ...), custom_call_target="tpu_custom_call" | custom-call | tf_op jit(solution)/shard_map/mix/pallas_call | solution.py:372
  55.0 1.6 %finish.1 = (bf16[256,256]{1,0:T(8,128)(2,1)}, bf16[256,256]{1,0:T(8,128)(2,1)}) custom-call(bf16[256,256]{1,0:T(8,128)(2,1)S(1)} %get-tuple-element.7.gqb, f32[2,256,128]{2,1,0:T(8,128)S(1)} %get-tuple-element.8.gc, f32[16,8,256]{2,1,0:T(8,128)S(1)} %get-tuple-element.9.ab, f32[16,8,256]{2,1,0:T(8,128)S(1)} %get-tuple-element.10.rb, ...), custom_call_target="tpu_custom_call" | custom-call | tf_op jit(solution)/shard_map/finish/pallas_call | solution.py:403

commit v3 on v2

--- a/solution.py
+++ b/solution.py
@@ -11,15 +11,16 @@
 LANES = 128
 UNROLL = 8
 NH = 2
+CHUNKS = ((0, 4, True), (4, 4, False))
 FIRST = ((0, 2), (0, 1), (0, 3), (1, 0), (1, 1))
 ARRIVED, SHARED, GATHERED, SUMMED, ADDED, SPREAD = range(6)
 EVENTS = (
     (0, 2, 0), (1, 2, 2), (0, 1, 0), (1, 2, 0), (1, 2, 1), (1, 2, 3), (2, 0, 0), (5, 0, 0), (2, 0, 4),
-    (1, 2, 5), (0, 3, 0), (1, 1, 0), (1, 1, 2), (2, 1, 0), (2, 1, 4), (1, 1, 1), (1, 1, 3), (1, 2, 4),
-    (2, 0, 1), (1, 3, 2), (1, 3, 0), (1, 3, 3), (1, 3, 1), (2, 0, 5), (1, 1, 5), (1, 1, 4), (1, 3, 5),
-    (2, 1, 1), (2, 1, 5), (0, 0, 0), (1, 3, 4), (2, 0, 2), (2, 0, 6), (1, 0, 2), (2, 1, 2), (2, 1, 6),
-    (1, 0, 0), (1, 0, 1), (1, 0, 3), (2, 0, 3), (3, 2, 0), (3, 1, 0), (3, 3, 0), (1, 0, 5), (2, 1, 7),
-    (3, 2, 1), (3, 1, 1), (3, 3, 1), (1, 0, 4), (3, 0, 0), (3, 0, 1), (4, 0, 0), (4, 0, 1), (4, 1, 0),
+    (1, 2, 5), (0, 3, 0), (1, 1, 0), (2, 1, 0), (2, 1, 4), (1, 1, 2), (1, 1, 1), (2, 0, 1), (1, 1, 3),
+    (1, 2, 4), (1, 3, 2), (1, 3, 0), (1, 3, 3), (2, 0, 5), (1, 3, 1), (1, 1, 5), (2, 1, 1), (2, 1, 5),
+    (1, 1, 4), (1, 3, 5), (0, 0, 0), (2, 0, 2), (2, 0, 6), (1, 3, 4), (2, 1, 2), (2, 1, 6), (1, 0, 2),
+    (1, 0, 0), (2, 0, 3), (3, 2, 0), (3, 1, 0), (3, 3, 0), (1, 0, 3), (1, 0, 1), (2, 1, 7), (3, 2, 1),
+    (3, 1, 1), (3, 3, 1), (1, 0, 5), (1, 0, 4), (4, 0, 0), (4, 0, 1), (3, 0, 0), (3, 0, 1), (4, 1, 0),
     (4, 1, 1),
 )
 
@@ -71,14 +72,13 @@
         pltpu.make_async_copy(r_hbm, r_ref, lsem.at[7]),
         pltpu.make_async_copy(a_hbm, a_ref, lsem.at[8]),
     ]
-    for c in locals_ + poles_in:
-        c.start()
-
     barrier = pltpu.get_barrier_semaphore()
     peers = [at_z(d) for d in range(1, NZ)] + [at_y(1), at_y(-1)]
     peers += [at_ctx(d) for d in range(1, NCTX)]
     for p in peers:
         pl.semaphore_signal(barrier, inc=1, device_id=p, device_id_type=MESH)
+    for c in locals_ + poles_in:
+        c.start()
     pl.semaphore_wait(barrier, len(peers))
 
     def rcopy(src, dst, ssem, rsem, dev):
@@ -87,7 +87,7 @@
         )
 
     def spread(dy):
-        for o in range(1, NZ):
+        for o in (4, 3, 5, 2, 6, 1, 7):
             zz = (z - o + NZ) % NZ
             row = (((y + dy) % NY) * NZ + zz) * NCTX + ctx
             rcopy(w_hbm.at[row], wbuf.at[dy, ctx, o], asend.at[dy], arecv.at[dy], at_z(-o)).start()
@@ -142,11 +142,11 @@
             xcopy(dy, 5).start()
         xcopy(dy, 7 + k).start()
 
-    half = tok // NH
-    quarter = half // 2
+    eighth = tok // 8
 
     def rows(h):
-        return pl.ds(h * half, half)
+        first, n, _ = CHUNKS[h]
+        return pl.ds(first * eighth, n * eighth)
 
     def gcopy(h, k):
         up = k < 4
@@ -159,7 +159,7 @@
         )
 
     def last(h):
-        return 3 if h < NH // 2 else 7
+        return 3 if CHUNKS[h][2] else 7
 
     def gather0(h):
         gcopy(h, 0).start()
@@ -209,11 +209,12 @@
         )
 
     def quart(h, side):
-        return pl.ds(h * half + side * quarter, quarter)
+        first, n, _ = CHUNKS[h]
+        return pl.ds(first * eighth + side * (n * eighth // 2), n * eighth // 2)
 
     def far(h, side):
         return rcopy(
-            pbuf.at[2, quart(h, side)], hbuf.at[side, h],
+            pbuf.at[2, quart(h, side)], hbuf.at[side, quart(h, 0)],
             ysend.at[0, side, h], yrecv.at[0, side, h], at_y(1 - 2 * side),
         )
 
@@ -234,7 +235,7 @@
 
     def added(h, side):
         far(h, side).wait_recv()
-        pbuf[1 + 2 * side, quart(h, side)] += hbuf[side, h]
+        pbuf[1 + 2 * side, quart(h, side)] += hbuf[side, quart(h, 0)]
         near(h, side, 1).start()
 
     here = False
@@ -378,7 +379,7 @@
             pltpu.VMEM((NZ, tok, wid), bf16),
             pltpu.VMEM((NY, NCTX, NZ, chunk, wid), bf16),
             pltpu.VMEM((NY, tok, wid), f32),
-            pltpu.VMEM((2, NH, tok // NH // 2, wid), f32),
+            pltpu.VMEM((2, tok, wid), f32),
             pltpu.VMEM((2, tok, wid), f32),
             pltpu.VMEM((tok, wid), bf16),
             pltpu.VMEM((tok, wid), bf16),

time: 56.7 us -> 54.8 us (0.966)
  Pallas kernels: 56 us -> 54.1 us
    pallas_call x1, Pallas kernels: 54.4 us -> 52.5 us  [local(): pl.pallas_call(kernel, out_shape=(full, jax.ShapeDtypeStruct((wid // LANE...]
where the time goes in v3:
time: 54.8 us; the launch traced here: 54.7 us
  Pallas kernels  54.1 us (99%)
  between operations  0.64 us (1%)
    pallas_call x1, Pallas kernels, local(): pl.pallas_call(kernel, out_shape=(full, jax.ShapeDtypeStruct((wid // LANE...  52.5 us
    pallas_call x1, Pallas kernels, local(): pl.pallas_call(finish, out_shape=(full, full), in_specs=[vm] * 5, out_spe...  1.58 us

profile of v3, /device:TPU:1, one launch (start us, length us, event | category | flops | bytes accessed | tf_op | source)
XLA Modules:
  0.0 54.7 jit_solution(12931886481353642496)
XLA Ops:
  0.6 52.5 %mix.1 = (bf16[256,256]{1,0:T(8,128)(2,1)S(1)}, f32[2,256,128]{2,1,0:T(8,128)S(1)}, f32[16,8,256]{2,1,0:T(8,128)S(1)}, f32[16,8,256]{2,1,0:T(8,128)S(1)}, f32[16,8,256]{2,1,0:T(8,128)S(1)}) custom-call(bf16[256,256]{1,0:T(8,128)(2,1)} %g_hbm.1, bf16[256,32,256]{2,1,0:T(8,128)(2,1)} %bitcast.3, bf16[256,256]{1,0:T(8,128)(2,1)} %q_hbm.1, ...), custom_call_target="tpu_custom_call" | custom-call | tf_op jit(solution)/shard_map/mix/pallas_call | solution.py:373
  53.2 1.6 %finish.1 = (bf16[256,256]{1,0:T(8,128)(2,1)}, bf16[256,256]{1,0:T(8,128)(2,1)}) custom-call(bf16[256,256]{1,0:T(8,128)(2,1)S(1)} %get-tuple-element.7.gqb, f32[2,256,128]{2,1,0:T(8,128)S(1)} %get-tuple-element.8.gc, f32[16,8,256]{2,1,0:T(8,128)S(1)} %get-tuple-element.9.ab, f32[16,8,256]{2,1,0:T(8,128)S(1)} %get-tuple-element.10.rb, ...), custom_call_target="tpu_custom_call" | custom-call | tf_op jit(solution)/shard_map/finish/pallas_call | solution.py:404

commit v4 on v3

--- a/solution.py
+++ b/solution.py
@@ -15,13 +15,13 @@
 FIRST = ((0, 2), (0, 1), (0, 3), (1, 0), (1, 1))
 ARRIVED, SHARED, GATHERED, SUMMED, ADDED, SPREAD = range(6)
 EVENTS = (
-    (0, 2, 0), (1, 2, 2), (0, 1, 0), (1, 2, 0), (1, 2, 1), (1, 2, 3), (2, 0, 0), (5, 0, 0), (2, 0, 4),
-    (1, 2, 5), (0, 3, 0), (1, 1, 0), (2, 1, 0), (2, 1, 4), (1, 1, 2), (1, 1, 1), (2, 0, 1), (1, 1, 3),
-    (1, 2, 4), (1, 3, 2), (1, 3, 0), (1, 3, 3), (2, 0, 5), (1, 3, 1), (1, 1, 5), (2, 1, 1), (2, 1, 5),
-    (1, 1, 4), (1, 3, 5), (0, 0, 0), (2, 0, 2), (2, 0, 6), (1, 3, 4), (2, 1, 2), (2, 1, 6), (1, 0, 2),
-    (1, 0, 0), (2, 0, 3), (3, 2, 0), (3, 1, 0), (3, 3, 0), (1, 0, 3), (1, 0, 1), (2, 1, 7), (3, 2, 1),
-    (3, 1, 1), (3, 3, 1), (1, 0, 5), (1, 0, 4), (4, 0, 0), (4, 0, 1), (3, 0, 0), (3, 0, 1), (4, 1, 0),
-    (4, 1, 1),
+    (0, 2, 0), (1, 2, 2), (0, 1, 0), (1, 2, 0), (2, 0, 0), (5, 0, 0), (2, 0, 4), (1, 2, 1), (1, 2, 3),
+    (2, 1, 0), (2, 1, 4), (1, 2, 5), (0, 3, 0), (1, 1, 0), (2, 0, 1), (1, 1, 2), (1, 1, 1), (1, 1, 3),
+    (1, 2, 4), (1, 3, 2), (2, 0, 5), (1, 3, 0), (1, 3, 3), (2, 1, 1), (2, 1, 5), (1, 3, 1), (1, 1, 5),
+    (2, 0, 2), (2, 0, 6), (1, 1, 4), (1, 3, 5), (0, 0, 0), (2, 1, 2), (2, 1, 6), (1, 3, 4), (2, 0, 3),
+    (3, 2, 0), (3, 1, 0), (3, 3, 0), (1, 0, 2), (1, 0, 0), (2, 1, 7), (3, 2, 1), (3, 1, 1), (3, 3, 1),
+    (4, 0, 0), (4, 0, 1), (4, 1, 0), (4, 1, 1), (1, 0, 5), (1, 0, 4), (1, 0, 3), (1, 0, 1), (3, 0, 0),
+    (3, 0, 1),
 )
 
 
@@ -30,10 +30,16 @@
     return [p * s + row for p, s in zip(poles, state)]
 
 
+def total(terms):
+    while len(terms) > 1:
+        terms = [terms[m] + terms[m + 1] for m in range(0, len(terms), 2)]
+    return terms[0]
+
+
 def kernel(
     g_hbm, w_hbm, q_hbm, v_hbm, r_hbm, a_hbm,
-    gqb, gc, ab, rb, start,
-    gbuf, wbuf, pbuf, hbuf, rbuf, qbuf, vbuf, r_ref, a_ref,
+    gqb, yf, ab, start,
+    gc, rb, gbuf, wbuf, pbuf, hbuf, rbuf, qbuf, vbuf, r_ref, a_ref,
     m1, m2, m4, a7, bpow, sown, sall,
     lsem, asend, arecv, gsend, grecv, xsend, xrecv, ysend, yrecv, ssend, srecv,
 ):
@@ -299,6 +305,24 @@
     ]
     for s in states:
         s.start()
+    for col in range(0, wid, lanes):
+        cols = slice(col, col + lanes)
+        poles = [ab[n, :, cols] for n in range(modes)]
+        gains = [rb[n, :, cols] for n in range(modes)]
+
+        def second(k, state, poles=poles, gains=gains, col=col):
+            state = list(state)
+            for u in range(UNROLL):
+                j = steps - 1 - (k * UNROLL + u)
+                state = sweep(gc, j, state, poles, col)
+                yf[col // lanes, pl.ds(j, SEG, stride=steps)] = total(
+                    [g * t for g, t in zip(gains, state)]
+                )
+            return tuple(state)
+
+        own_ends = tuple(ends[(col // lanes) * modes + n] for n in range(modes))
+        lax.fori_loop(0, steps // UNROLL, second, own_ends)
+
     incoming = jnp.zeros((modes, wid), f32)
     for d in range(NCTX - 1, 0, -1):
         rcopy(sown, sall.at[d], ssend.at[d], srecv.at[d], at_ctx(d)).wait_recv()
@@ -308,7 +332,7 @@
     for t in range(len(ends)):
         n, col = t % modes, (t // modes) * lanes
         cols = slice(col, col + lanes)
-        start[n, :, cols] = ends[t] + a7[n, :, cols] * incoming[n : n + 1, cols]
+        start[n, :, cols] = rb[n, :, cols] * a7[n, :, cols] * incoming[n : n + 1, cols]
 
     for dy in range(NY):
         ref = block(dy, ctx, *full)
@@ -328,29 +352,26 @@
         s.wait_send()
 
 
-def finish(gqb, gc, ab, rb, start, gq_hbm, gi_hbm, yf, gib, sem):
+def finish(gqb, yf, ab, start, gq_hbm, gi_hbm, ys, gib, sem):
     modes, _, wid = ab.shape
-    steps = gqb.shape[0] // SEG
+    tok = gqb.shape[0]
+    steps = tok // SEG
     out_q = pltpu.make_async_copy(gqb, gq_hbm, sem.at[0])
     out_q.start()
     for col in range(0, wid, LANES):
         cols = slice(col, col + LANES)
         poles = [ab[n, :, cols] for n in range(modes)]
-        gains = [rb[n, :, cols] for n in range(modes)]
-
-        def second(k, state, poles=poles, gains=gains, col=col):
+
+        def third(k, state, poles=poles, col=col):
             state = list(state)
             for u in range(UNROLL):
-                j = steps - 1 - (k * UNROLL + u)
-                state = sweep(gc, j, state, poles, col)
-                terms = [gains[n] * state[n] for n in range(modes)]
-                while len(terms) > 1:
-                    terms = [terms[m] + terms[m + 1] for m in range(0, len(terms), 2)]
-                yf[col // LANES, pl.ds(j, SEG, stride=steps)] = terms[0]
+                at = pl.ds(steps - 1 - (k * UNROLL + u), SEG, stride=steps)
+                state = [p * t for p, t in zip(poles, state)]
+                ys[col // LANES, at] = yf[col // LANES, at] + total(state)
             return tuple(state)
 
-        lax.fori_loop(0, steps // UNROLL, second, tuple(start[n, :, cols] for n in range(modes)))
-        gib[:, cols] = yf[col // LANES].astype(gib.dtype)
+        lax.fori_loop(0, steps // UNROLL, third, tuple(start[n, :, cols] for n in range(modes)))
+        gib[:, cols] = ys[col // LANES].astype(gib.dtype)
     out_i = pltpu.make_async_copy(gib, gi_hbm, sem.at[1])
     out_i.start()
     out_q.wait()
@@ -372,10 +393,12 @@
     inputs = (out_grad, w, query_in, conv_out, residues.T, decay_rates.T)
     held = pl.pallas_call(
         kernel,
-        out_shape=(full, jax.ShapeDtypeStruct((wid // LANES, tok, LANES), f32), tall, tall, tall),
+        out_shape=(full, jax.ShapeDtypeStruct((wid // LANES, tok, LANES), f32), tall, tall),
         in_specs=[any_] * 6,
-        out_specs=(vm,) * 5,
+        out_specs=(vm,) * 4,
         scratch_shapes=[
+            pltpu.VMEM((wid // LANES, tok, LANES), f32),
+            table,
             pltpu.VMEM((NZ, tok, wid), bf16),
             pltpu.VMEM((NY, NCTX, NZ, chunk, wid), bf16),
             pltpu.VMEM((NY, tok, wid), f32),
@@ -404,7 +427,7 @@
     return pl.pallas_call(
         finish,
         out_shape=(full, full),
-        in_specs=[vm] * 5,
+        in_specs=[vm] * 4,
         out_specs=(any_, any_),
         scratch_shapes=[
             pltpu.VMEM((wid // LANES, tok, LANES), f32),

time: 54.8 us -> 54.1 us (0.987)
  Pallas kernels: 54.1 us -> 53.3 us
where the time goes in v4:
time: 54.1 us; the launch traced here: 54 us
  Pallas kernels  53.3 us (99%)
  between operations  0.64 us (1%)
    pallas_call x1, Pallas kernels, local(): pl.pallas_call(kernel, out_shape=(full, jax.ShapeDtypeStruct((wid // LANE...  52.1 us
    pallas_call x1, Pallas kernels, local(): pl.pallas_call(finish, out_shape=(full, full), in_specs=[vm] * 4, out_spe...  1.24 us

profile of v4, /device:TPU:1, one launch (start us, length us, event | category | flops | bytes accessed | tf_op | source)
XLA Modules:
  0.0 54.0 jit_solution(5161507003590899635)
XLA Ops:
  0.6 52.1 %mix.1 = (bf16[256,256]{1,0:T(8,128)(2,1)S(1)}, f32[2,256,128]{2,1,0:T(8,128)S(1)}, f32[16,8,256]{2,1,0:T(8,128)S(1)}, f32[16,8,256]{2,1,0:T(8,128)S(1)}) custom-call(bf16[256,256]{1,0:T(8,128)(2,1)} %g_hbm.1, bf16[256,32,256]{2,1,0:T(8,128)(2,1)} %bitcast.3, bf16[256,256]{1,0:T(8,128)(2,1)} %q_hbm.1, bf16[256,256]{1,0:T(8,128)(2,1)} %v_hbm.1, ...), custom_call_target="tpu_custom_call" | custom-call | tf_op jit(solution)/shard_map/mix/pallas_call | solution.py:394
  52.7 1.2 %finish.1 = (bf16[256,256]{1,0:T(8,128)(2,1)}, bf16[256,256]{1,0:T(8,128)(2,1)}) custom-call(bf16[256,256]{1,0:T(8,128)(2,1)S(1)} %get-tuple-element.6.gqb, f32[2,256,128]{2,1,0:T(8,128)S(1)} %get-tuple-element.7.yf, f32[16,8,256]{2,1,0:T(8,128)S(1)} %get-tuple-element.8.ab, f32[16,8,256]{2,1,0:T(8,128)S(1)} %get-tuple-element.9.start), custom_call_target="tpu_custom_call" | custom-call | tf_op jit(solution)/shard_map/finish/pallas_call | solution.py:427

commit v5 on v4

--- a/solution.py
+++ b/solution.py
@@ -21,7 +21,6 @@
     (2, 0, 2), (2, 0, 6), (1, 1, 4), (1, 3, 5), (0, 0, 0), (2, 1, 2), (2, 1, 6), (1, 3, 4), (2, 0, 3),
     (3, 2, 0), (3, 1, 0), (3, 3, 0), (1, 0, 2), (1, 0, 0), (2, 1, 7), (3, 2, 1), (3, 1, 1), (3, 3, 1),
     (4, 0, 0), (4, 0, 1), (4, 1, 0), (4, 1, 1), (1, 0, 5), (1, 0, 4), (1, 0, 3), (1, 0, 1), (3, 0, 0),
-    (3, 0, 1),
 )
 
 
@@ -207,10 +206,10 @@
         b = b * b
     bpow[...] = b
 
-    def partial(dy, h):
-        g = jnp.concatenate([gbuf[o, rows(h)] for o in range(NZ)], axis=1)
+    def partial(dy, part):
+        g = jnp.concatenate([gbuf[o, part] for o in range(NZ)], axis=1)
         w = jnp.concatenate([wbuf[dy, :, o].reshape(wid, wid) for o in range(NZ)], axis=1)
-        pbuf[dy, rows(h)] = lax.dot_general(
+        pbuf[dy, part] = lax.dot_general(
             g, w, (((1,), (1,)), ((), ())), preferred_element_type=f32
         )
 
@@ -232,7 +231,7 @@
         )
 
     def summed(dy, h):
-        partial(dy, h)
+        partial(dy, rows(h) if dy else pl.ds(0, tok))
         if dy == 2:
             far(h, 0).start()
             far(h, 1).start()

time: 54.1 us -> 54 us (level)
  no operation moved by 1% of the time
where the time goes in v5:
time: 54 us; the launch traced here: 53.9 us
  Pallas kernels  53.3 us (99%)
  between operations  0.64 us (1%)
    pallas_call x1, Pallas kernels, local(): pl.pallas_call(kernel, out_shape=(full, jax.ShapeDtypeStruct((wid // LANE...  52.1 us
    pallas_call x1, Pallas kernels, local(): pl.pallas_call(finish, out_shape=(full, full), in_specs=[vm] * 4, out_spe...  1.24 us

profile of v5, /device:TPU:1, one launch (start us, length us, event | category | flops | bytes accessed | tf_op | source)
XLA Modules:
  0.0 53.9 jit_solution(2703178660555338939)
XLA Ops:
  0.6 52.1 %mix.1 = (bf16[256,256]{1,0:T(8,128)(2,1)S(1)}, f32[2,256,128]{2,1,0:T(8,128)S(1)}, f32[16,8,256]{2,1,0:T(8,128)S(1)}, f32[16,8,256]{2,1,0:T(8,128)S(1)}) custom-call(bf16[256,256]{1,0:T(8,128)(2,1)} %g_hbm.1, bf16[256,32,256]{2,1,0:T(8,128)(2,1)} %bitcast.3, bf16[256,256]{1,0:T(8,128)(2,1)} %q_hbm.1, bf16[256,256]{1,0:T(8,128)(2,1)} %v_hbm.1, ...), custom_call_target="tpu_custom_call" | custom-call | tf_op jit(solution)/shard_map/mix/pallas_call | solution.py:393
  52.7 1.2 %finish.1 = (bf16[256,256]{1,0:T(8,128)(2,1)}, bf16[256,256]{1,0:T(8,128)(2,1)}) custom-call(bf16[256,256]{1,0:T(8,128)(2,1)S(1)} %get-tuple-element.6.gqb, f32[2,256,128]{2,1,0:T(8,128)S(1)} %get-tuple-element.7.yf, f32[16,8,256]{2,1,0:T(8,128)S(1)} %get-tuple-element.8.ab, f32[16,8,256]{2,1,0:T(8,128)S(1)} %get-tuple-element.9.start), custom_call_target="tpu_custom_call" | custom-call | tf_op jit(solution)/shard_map/finish/pallas_call | solution.py:426
